TPU v7x, 32 devices: a whole 2x2x4 slice. The times are simulated.
32 devices in a mesh: fsdp: 16 (over z, y, core), ctx: 2 (over x).
Axes of the slice: x: 2, y: 2, z: 4, core: 2. Of those that a mesh axis runs over, the one named last changes fastest.
Arguments:
- tokens: bfloat16 [4096, 1024], P(('fsdp', 'ctx')), may hold values from -6 to 6
- cotangent: bfloat16 [4096, 1024], P(('fsdp', 'ctx')), may hold values from -6 to 6
- seq_lengths: int32 [16, 4], P('fsdp'), may hold values from 1 to 128, 256 in all within a row
- query_key_value_weight: float32 [1024, 4096], P(('fsdp', 'ctx')), may hold values from -0.1875 to 0.1875
- first_moment_projection: float32 [1024, 4096], P(('fsdp', 'ctx')), may hold values from -12 to 12
- second_moment_projection: float32 [1024, 4096], P(('fsdp', 'ctx')), may hold values from 1 to 100
- w_out: float32 [2048, 1024], P(('fsdp', 'ctx')), may hold values from -0.625 to 0.625
- m_out: float32 [2048, 1024], P(('fsdp', 'ctx')), may hold values from -12 to 12
- v_out: float32 [2048, 1024], P(('fsdp', 'ctx')), may hold values from 1 to 100
- w_gateup: float32 [1024, 6144], P(('fsdp', 'ctx')), may hold values from -0.1875 to 0.1875
- m_gateup: float32 [1024, 6144], P(('fsdp', 'ctx')), may hold values from -12 to 12
- v_gateup: float32 [1024, 6144], P(('fsdp', 'ctx')), may hold values from 1 to 100
- w_down: float32 [3072, 1024], P(('fsdp', 'ctx')), may hold values from -0.109375 to 0.109375
- m_down: float32 [3072, 1024], P(('fsdp', 'ctx')), may hold values from -12 to 12
- v_down: float32 [3072, 1024], P(('fsdp', 'ctx')), may hold values from 1 to 100
- attn_gain: float32 [1024], replicated, may hold values from 0.5 to 1.5
- m_attn_gain: float32 [1024], replicated, may hold values from -120 to 120
- v_attn_gain: float32 [1024], replicated, may hold values from 100 to 10000
- mlp_gain: float32 [1024], replicated, may hold values from 0.5 to 1.5
- m_mlp_gain: float32 [1024], replicated, may hold values from -120 to 120
- v_mlp_gain: float32 [1024], replicated, may hold values from 100 to 10000
- q_gain: float32 [128], replicated, may hold values from 0.5 to 1.5
- m_q_gain: float32 [128], replicated, may hold values from -120 to 120
- v_q_gain: float32 [128], replicated, may hold values from 100 to 10000
- k_gain: float32 [128], replicated, may hold values from 0.5 to 1.5
- m_k_gain: float32 [128], replicated, may hold values from -120 to 120
- v_k_gain: float32 [128], replicated, may hold values from 100 to 10000
Outputs:
- output: bfloat16 [4096, 1024], P(('fsdp', 'ctx'))
- grad_tokens: float32 [4096, 1024], P(('fsdp', 'ctx'))
- grad_qkv: float32 [1024, 4096], P(('fsdp', 'ctx'))
- new_w_qkv: float32 [1024, 4096], P(('fsdp', 'ctx'))
- new_m_qkv: float32 [1024, 4096], P(('fsdp', 'ctx'))
- new_v_qkv: float32 [1024, 4096], P(('fsdp', 'ctx'))
- grad_out: float32 [2048, 1024], P(('fsdp', 'ctx'))
- new_w_out: float32 [2048, 1024], P(('fsdp', 'ctx'))
- new_m_out: float32 [2048, 1024], P(('fsdp', 'ctx'))
- new_v_out: float32 [2048, 1024], P(('fsdp', 'ctx'))
- grad_gateup: float32 [1024, 6144], P(('fsdp', 'ctx'))
- new_w_gateup: float32 [1024, 6144], P(('fsdp', 'ctx'))
- new_m_gateup: float32 [1024, 6144], P(('fsdp', 'ctx'))
- new_v_gateup: float32 [1024, 6144], P(('fsdp', 'ctx'))
- grad_down: float32 [3072, 1024], P(('fsdp', 'ctx'))
- new_w_down: float32 [3072, 1024], P(('fsdp', 'ctx'))
- new_m_down: float32 [3072, 1024], P(('fsdp', 'ctx'))
- new_v_down: float32 [3072, 1024], P(('fsdp', 'ctx'))
- grad_attn_gain: float32 [1024], replicated
- new_attn_gain: float32 [1024], replicated
- new_m_attn_gain: float32 [1024], replicated
- new_v_attn_gain: float32 [1024], replicated
- grad_mlp_gain: float32 [1024], replicated
- new_mlp_gain: float32 [1024], replicated
- new_m_mlp_gain: float32 [1024], replicated
- new_v_mlp_gain: float32 [1024], replicated
- grad_q_gain: float32 [128], replicated
- new_q_gain: float32 [128], replicated
- new_m_q_gain: float32 [128], replicated
- new_v_q_gain: float32 [128], replicated
- grad_k_gain: float32 [128], replicated
- new_k_gain: float32 [128], replicated
- new_m_k_gain: float32 [128], replicated
- new_v_k_gain: float32 [128], replicated
Inputs may be any that keep to these rules, and one draw needn't show every extreme that they name: `seq_lengths`: each row holds the lengths of the 4 sequences packed one after another into a group; a row sums to 256 and its largest entry is exactly 128.
All inputs are finite; a program needn't handle non-finite values.
Results may differ from a plain program's by a relative error of at most 0.025.
Values may be sent and summed in bfloat16 or wider, within the bound.
No kernel may reach another device: no remote copies, remote signals or barrier semaphores. Data moves between devices by JAX's collectives and lax.ppermute only.
A program may use at most 256 MiB of HBM per device.

v0:
```python
import math
import jax
import jax.numpy as jnp
from jax import lax
from jax.sharding import PartitionSpec as P

QUERY_HEADS = 16
KEY_VALUE_HEADS = 8
HEAD_WIDTH = 128
FF = 3072
STEP = 3
NORM_EPS = 1e-06
ROPE_BASE = 1000000.0
NEG_LARGE = -1e30
BETA_ONE = 0.9
BETA_TWO = 0.95
ADAM_EPS = 1e-08
MATRIX_RATE = 0.04
GAIN_RATE = 0.2
MATRIX_DECAY = 0.1


def seq_place(lengths, positions):
    ends = jnp.cumsum(lengths)
    passed = ends[None, :] <= positions[:, None]
    segment = jnp.sum(passed.astype(jnp.int32), axis=1)
    start = jnp.sum(jnp.where(passed, lengths[None, :], 0), axis=1)
    return (segment, positions - start)


def rope_tables(offsets, head_size):
    half_size = head_size // 2
    freqs = ROPE_BASE ** (-(2.0 * jnp.arange(half_size, dtype=jnp.float32)) / head_size)
    angles = offsets.astype(jnp.float32)[:, None] * freqs[None, :]
    cosine = jnp.concatenate([jnp.cos(angles), jnp.cos(angles)], axis=1)[:, None, :]
    sine = jnp.concatenate([jnp.sin(angles), jnp.sin(angles)], axis=1)[:, None, :]
    return (cosine, sine)


def rope_apply(values, cosine, sine):
    half_size = values.shape[-1] // 2
    rotated = jnp.concatenate([-values[..., half_size:], values[..., :half_size]], axis=-1)
    return values * cosine + rotated * sine


def rope_back(grads, cosine, sine):
    half_size = grads.shape[-1] // 2
    scaled = grads * sine
    return grads * cosine + jnp.concatenate(
        [scaled[..., half_size:], -scaled[..., :half_size]], axis=-1
    )


def norm_back(grads, values, inv_rms, gain):
    scaled = grads * gain
    return inv_rms * scaled - values * (inv_rms * inv_rms * inv_rms) * jnp.mean(
        scaled * values, axis=-1, keepdims=True
    )


def adamw(weight, first, second, grads, rate, decay):
    new_first = BETA_ONE * first + (1.0 - BETA_ONE) * grads
    new_second = BETA_TWO * second + (1.0 - BETA_TWO) * grads * grads
    first_hat = new_first / (1.0 - BETA_ONE**STEP)
    second_hat = new_second / (1.0 - BETA_TWO**STEP)
    new_weight = weight - rate * (first_hat / (jnp.sqrt(second_hat) + ADAM_EPS) + decay * weight)
    return (new_weight, new_first, new_second)


def reduce_mlp(grad_gateup, grad_down):
    return (
        lax.psum_scatter(grad_gateup, ("fsdp", "ctx"), scatter_dimension=0, tiled=True),
        lax.psum_scatter(grad_down, ("fsdp", "ctx"), scatter_dimension=0, tiled=True),
    )


def reduce_attn(grad_qkv, grad_out):
    return (
        lax.psum_scatter(grad_qkv, ("fsdp", "ctx"), scatter_dimension=0, tiled=True),
        lax.psum_scatter(grad_out, ("fsdp", "ctx"), scatter_dimension=0, tiled=True),
    )


def local(
    tokens,
    cotangent,
    seq_lengths,
    query_key_value_weight,
    first_moment_projection,
    second_moment_projection,
    w_out,
    m_out,
    v_out,
    w_gateup,
    m_gateup,
    v_gateup,
    w_down,
    m_down,
    v_down,
    attn_gain,
    m_attn_gain,
    v_attn_gain,
    mlp_gain,
    m_mlp_gain,
    v_mlp_gain,
    q_gain,
    m_q_gain,
    v_q_gain,
    k_gain,
    m_k_gain,
    v_k_gain,
):
    token_rows = tokens.shape[0]
    ctx_index = lax.axis_index("ctx")
    ctx_count = lax.axis_size("ctx")
    reach_back = ctx_count // 2
    rows_in_window = (reach_back + 1) * token_rows
    heads_per_group = QUERY_HEADS // KEY_VALUE_HEADS
    key_value_width = KEY_VALUE_HEADS * HEAD_WIDTH
    score_scale = 1.0 / math.sqrt(HEAD_WIDTH)
    lengths = seq_lengths[0]
    q_places = ctx_index * token_rows + jnp.arange(token_rows, dtype=jnp.int32)
    q_segment, q_offset = seq_place(lengths, q_places)
    k_places = (ctx_index - reach_back) * token_rows + jnp.arange(rows_in_window, dtype=jnp.int32)
    k_segment, k_unused = seq_place(lengths, k_places)
    k_segment = jnp.where(k_places >= 0, k_segment, -1)
    allowed = (q_segment[:, None] == k_segment[None, :]) & (k_places[None, :] <= q_places[:, None])
    cosine, sine = rope_tables(q_offset, HEAD_WIDTH)
    attn_w, out_w = (
        lax.all_gather(
            query_key_value_weight.astype(jnp.bfloat16), ("fsdp", "ctx"), axis=0, tiled=True
        ),
        lax.all_gather(w_out.astype(jnp.bfloat16), ("fsdp", "ctx"), axis=0, tiled=True),
    )
    gateup_w, down_w = (
        lax.all_gather(w_gateup.astype(jnp.bfloat16), ("fsdp", "ctx"), axis=0, tiled=True),
        lax.all_gather(w_down.astype(jnp.bfloat16), ("fsdp", "ctx"), axis=0, tiled=True),
    )
    tok_float = tokens.astype(jnp.float32)
    inv_one = lax.rsqrt(jnp.mean(tok_float * tok_float, axis=1, keepdims=True) + NORM_EPS)
    normed_one = (tok_float * inv_one * attn_gain).astype(jnp.bfloat16)
    projected_rows = jnp.dot(normed_one, attn_w, preferred_element_type=jnp.float32)
    query = projected_rows[:, : QUERY_HEADS * HEAD_WIDTH].reshape(
        token_rows, QUERY_HEADS, HEAD_WIDTH
    )
    unrotated_key = projected_rows[
        :, QUERY_HEADS * HEAD_WIDTH : QUERY_HEADS * HEAD_WIDTH + key_value_width
    ].reshape(token_rows, KEY_VALUE_HEADS, HEAD_WIDTH)
    unprojected_value = projected_rows[:, QUERY_HEADS * HEAD_WIDTH + key_value_width :]
    inv_q = lax.rsqrt(jnp.mean(query * query, axis=2, keepdims=True) + NORM_EPS)
    inv_k = lax.rsqrt(jnp.mean(unrotated_key * unrotated_key, axis=2, keepdims=True) + NORM_EPS)
    rotated_query = rope_apply(query * inv_q * q_gain, cosine, sine).astype(jnp.bfloat16)
    k_rot = rope_apply(unrotated_key * inv_k * k_gain, cosine, sine).astype(jnp.bfloat16)
    kv_own = jnp.concatenate(
        [k_rot.reshape(token_rows, key_value_width), unprojected_value.astype(jnp.bfloat16)], axis=1
    )
    kv_group = lax.all_gather(kv_own, "ctx", axis=0, tiled=True)
    padded = jnp.concatenate(
        [jnp.zeros((reach_back * token_rows, 2 * key_value_width), jnp.bfloat16), kv_group], axis=0
    )
    key_value_window = lax.dynamic_slice_in_dim(padded, ctx_index * token_rows, rows_in_window, 0)
    key_window = key_value_window[:, :key_value_width].reshape(
        rows_in_window, KEY_VALUE_HEADS, HEAD_WIDTH
    )
    value_window = key_value_window[:, key_value_width:].reshape(
        rows_in_window, KEY_VALUE_HEADS, HEAD_WIDTH
    )
    query_four_dims = rotated_query.reshape(
        token_rows, KEY_VALUE_HEADS, heads_per_group, HEAD_WIDTH
    )
    scores = (
        jnp.einsum(
            "tkgd,jkd->kgtj", query_four_dims, key_window, preferred_element_type=jnp.float32
        )
        * score_scale
    )
    scores = jnp.where(allowed, scores, NEG_LARGE)
    peak = jnp.max(scores, axis=3, keepdims=True)
    expd = jnp.exp(scores - peak)
    totals = jnp.sum(expd, axis=3, keepdims=True)
    log_total = peak + jnp.log(totals)
    probs_half = jnp.exp(scores - log_total).astype(jnp.bfloat16)
    attn_half = jnp.einsum(
        "kgtj,jkd->tkgd", probs_half, value_window, preferred_element_type=jnp.float32
    )
    attn_half = attn_half.reshape(token_rows, QUERY_HEADS * HEAD_WIDTH).astype(jnp.bfloat16)
    resid = tok_float + jnp.dot(attn_half, out_w, preferred_element_type=jnp.float32)
    inv_two = lax.rsqrt(jnp.mean(resid * resid, axis=1, keepdims=True) + NORM_EPS)
    normed_two = (resid * inv_two * mlp_gain).astype(jnp.bfloat16)
    gate_up = jnp.dot(normed_two, gateup_w, preferred_element_type=jnp.float32)
    gate = gate_up[:, :FF]
    upper = gate_up[:, FF:]
    sigm = jax.nn.sigmoid(gate)
    active = gate * sigm
    hidden = (active * upper).astype(jnp.bfloat16)
    output = (resid + jnp.dot(hidden, down_w, preferred_element_type=jnp.float32)).astype(
        jnp.bfloat16
    )
    gateup_back, down_back = (
        lax.all_gather(w_gateup.astype(jnp.bfloat16), ("fsdp", "ctx"), axis=0, tiled=True),
        lax.all_gather(w_down.astype(jnp.bfloat16), ("fsdp", "ctx"), axis=0, tiled=True),
    )
    grad_down = jnp.dot(hidden.T, cotangent, preferred_element_type=jnp.float32)
    grad_hidden = jnp.dot(cotangent, down_back.T, preferred_element_type=jnp.float32)
    grad_gate = grad_hidden * upper * (sigm * (1.0 + gate * (1.0 - sigm)))
    grad_upper = grad_hidden * active
    grad_gu = jnp.concatenate([grad_gate, grad_upper], axis=1).astype(jnp.bfloat16)
    grad_gateup = jnp.dot(normed_two.T, grad_gu, preferred_element_type=jnp.float32)
    share_gateup, share_down = reduce_mlp(grad_gateup, grad_down)
    grad_n_two = jnp.dot(grad_gu, gateup_back.T, preferred_element_type=jnp.float32)
    gain_two = jnp.sum(grad_n_two * resid * inv_two, axis=0)
    grad_resid = cotangent.astype(jnp.float32) + norm_back(grad_n_two, resid, inv_two, mlp_gain)
    resid_half = grad_resid.astype(jnp.bfloat16)
    attn_back, out_back = (
        lax.all_gather(
            query_key_value_weight.astype(jnp.bfloat16), ("fsdp", "ctx"), axis=0, tiled=True
        ),
        lax.all_gather(w_out.astype(jnp.bfloat16), ("fsdp", "ctx"), axis=0, tiled=True),
    )
    grad_out = jnp.dot(attn_half.T, resid_half, preferred_element_type=jnp.float32)
    attention_gradient = jnp.dot(resid_half, out_back.T, preferred_element_type=jnp.float32).astype(
        jnp.bfloat16
    )
    attention_gradient = attention_gradient.reshape(
        token_rows, KEY_VALUE_HEADS, heads_per_group, HEAD_WIDTH
    )
    grad_probs = jnp.einsum(
        "tkgd,jkd->kgtj", attention_gradient, value_window, preferred_element_type=jnp.float32
    )
    probs_full = jnp.exp(scores - log_total)
    grad_scores = probs_full * (
        grad_probs - jnp.sum(probs_full * grad_probs, axis=3, keepdims=True)
    )
    scores_half = (grad_scores * score_scale).astype(jnp.bfloat16)
    grad_qrot = jnp.einsum(
        "kgtj,jkd->tkgd", scores_half, key_window, preferred_element_type=jnp.float32
    ).reshape(token_rows, QUERY_HEADS, HEAD_WIDTH)
    grad_kwin = jnp.einsum(
        "kgtj,tkgd->jkd", scores_half, query_four_dims, preferred_element_type=jnp.float32
    ).reshape(rows_in_window, key_value_width)
    grad_vwin = jnp.einsum(
        "kgtj,tkgd->jkd", probs_half, attention_gradient, preferred_element_type=jnp.float32
    ).reshape(rows_in_window, key_value_width)
    grad_window = jnp.concatenate([grad_kwin, grad_vwin], axis=1)
    placed = jnp.zeros(((reach_back + ctx_count) * token_rows, 2 * key_value_width), jnp.float32)
    placed = lax.dynamic_update_slice_in_dim(placed, grad_window, ctx_index * token_rows, 0)
    local_gradient = lax.psum_scatter(
        placed[reach_back * token_rows :].astype(jnp.bfloat16),
        "ctx",
        scatter_dimension=0,
        tiled=True,
    ).astype(jnp.float32)
    rotated_key_gradient = local_gradient[:, :key_value_width].reshape(
        token_rows, KEY_VALUE_HEADS, HEAD_WIDTH
    )
    grad_value = local_gradient[:, key_value_width:]
    grad_qn = rope_back(grad_qrot, cosine, sine)
    grad_kn = rope_back(rotated_key_gradient, cosine, sine)
    gain_q = jnp.sum(grad_qn * query * inv_q, axis=(0, 1))
    gain_k = jnp.sum(grad_kn * unrotated_key * inv_k, axis=(0, 1))
    grad_query = norm_back(grad_qn, query, inv_q, q_gain).reshape(
        token_rows, QUERY_HEADS * HEAD_WIDTH
    )
    grad_key = norm_back(grad_kn, unrotated_key, inv_k, k_gain).reshape(token_rows, key_value_width)
    grad_proj = jnp.concatenate([grad_query, grad_key, grad_value], axis=1).astype(jnp.bfloat16)
    grad_qkv = jnp.dot(normed_one.T, grad_proj, preferred_element_type=jnp.float32)
    grad_n_one = jnp.dot(grad_proj, attn_back.T, preferred_element_type=jnp.float32)
    gain_one = jnp.sum(grad_n_one * tok_float * inv_one, axis=0)
    grad_tokens = grad_resid + norm_back(grad_n_one, tok_float, inv_one, attn_gain)
    share_qkv, share_out = reduce_attn(grad_qkv, grad_out)
    g_one, g_two, g_q, g_k = lax.psum((gain_one, gain_two, gain_q, gain_k), ("fsdp", "ctx"))
    up_qkv = adamw(
        query_key_value_weight,
        first_moment_projection,
        second_moment_projection,
        share_qkv,
        MATRIX_RATE,
        MATRIX_DECAY,
    )
    up_out = adamw(w_out, m_out, v_out, share_out, MATRIX_RATE, MATRIX_DECAY)
    up_gateup = adamw(w_gateup, m_gateup, v_gateup, share_gateup, MATRIX_RATE, MATRIX_DECAY)
    up_down = adamw(w_down, m_down, v_down, share_down, MATRIX_RATE, MATRIX_DECAY)
    up_one = adamw(attn_gain, m_attn_gain, v_attn_gain, g_one, GAIN_RATE, 0.0)
    up_two = adamw(mlp_gain, m_mlp_gain, v_mlp_gain, g_two, GAIN_RATE, 0.0)
    up_q = adamw(q_gain, m_q_gain, v_q_gain, g_q, GAIN_RATE, 0.0)
    up_k = adamw(k_gain, m_k_gain, v_k_gain, g_k, GAIN_RATE, 0.0)
    return (
        output,
        grad_tokens,
        share_qkv,
        up_qkv[0],
        up_qkv[1],
        up_qkv[2],
        share_out,
        up_out[0],
        up_out[1],
        up_out[2],
        share_gateup,
        up_gateup[0],
        up_gateup[1],
        up_gateup[2],
        share_down,
        up_down[0],
        up_down[1],
        up_down[2],
        g_one,
        up_one[0],
        up_one[1],
        up_one[2],
        g_two,
        up_two[0],
        up_two[1],
        up_two[2],
        g_q,
        up_q[0],
        up_q[1],
        up_q[2],
        g_k,
        up_k[0],
        up_k[1],
        up_k[2],
    )


def solution(mesh):
    in_specs = (
        P(("fsdp", "ctx"), None),
        P(("fsdp", "ctx"), None),
        P("fsdp", None),
        P(("fsdp", "ctx"), None),
        P(("fsdp", "ctx"), None),
        P(("fsdp", "ctx"), None),
        P(("fsdp", "ctx"), None),
        P(("fsdp", "ctx"), None),
        P(("fsdp", "ctx"), None),
        P(("fsdp", "ctx"), None),
        P(("fsdp", "ctx"), None),
        P(("fsdp", "ctx"), None),
        P(("fsdp", "ctx"), None),
        P(("fsdp", "ctx"), None),
        P(("fsdp", "ctx"), None),
        P(),
        P(),
        P(),
        P(),
        P(),
        P(),
        P(),
        P(),
        P(),
        P(),
        P(),
        P(),
    )
    out_specs = (
        P(("fsdp", "ctx"), None),
        P(("fsdp", "ctx"), None),
        P(("fsdp", "ctx"), None),
        P(("fsdp", "ctx"), None),
        P(("fsdp", "ctx"), None),
        P(("fsdp", "ctx"), None),
        P(("fsdp", "ctx"), None),
        P(("fsdp", "ctx"), None),
        P(("fsdp", "ctx"), None),
        P(("fsdp", "ctx"), None),
        P(("fsdp", "ctx"), None),
        P(("fsdp", "ctx"), None),
        P(("fsdp", "ctx"), None),
        P(("fsdp", "ctx"), None),
        P(("fsdp", "ctx"), None),
        P(("fsdp", "ctx"), None),
        P(("fsdp", "ctx"), None),
        P(("fsdp", "ctx"), None),
        P(),
        P(),
        P(),
        P(),
        P(),
        P(),
        P(),
        P(),
        P(),
        P(),
        P(),
        P(),
        P(),
        P(),
        P(),
        P(),
    )
    return jax.shard_map(local, mesh=mesh, in_specs=in_specs, out_specs=out_specs, check_vma=False)
```

profile of v0, /device:TPU:11, one launch (start us, length us, event | category | flops | bytes accessed | tf_op | source)
XLA Modules:
  0.0 1383.0 jit_solution(14045614941543385687)
XLA Ops:
  7.3 1.8 convert_element_type.83
  10.0 1.2 fusion.66
  13.0 1.1 fusion.29
  15.3 74.9 %all-gather.6.cloned.1.call-done = bf16[1024,4096]{1,0:T(8,128)(2,1)} async-done(((bf16[32,4096]{1,0:T(8,128)(2,1)}), bf16[1024,4096]{1,0:T(8,128)(2,1)}) %all-gather.6.cloned.1.call-update) | async-done | bytes 8388624 | tf_op jit(solution)/shard_map/all_gather | solution.py:130
  90.2 4.7 fusion.61
  97.7 1.0 multiply_multiply_fusion.4
  98.9 1.0 maximum_multiply_fusion.1
  101.9 1.7 convert_element_type.93
  103.6 1.9 convert_element_type.95
  106.8 1.4 compare_and_fusion
  110.2 10.2 all-gather.8.cloned.1.call-done
  120.4 1.4 fusion.38
  123.4 0.9 copy-done.1
  124.9 62.0 %all-gather.10.cloned.1.call-done = bf16[2048,1024]{1,0:T(8,128)(2,1)} async-done(((bf16[64,1024]{1,0:T(8,128)(2,1)}), bf16[2048,1024]{1,0:T(8,128)(2,1)}) %all-gather.10.cloned.1.call-update) | async-done | bytes 4194320 | tf_op jit(solution)/shard_map/all_gather | solution.py:133
  186.9 3.0 multiply_reduce_fusion.5
  190.6 93.7 %all-gather.12.cloned.1.call-done = bf16[1024,6144]{1,0:T(8,128)(2,1)} async-done(((bf16[32,6144]{1,0:T(8,128)(2,1)}), bf16[1024,6144]{1,0:T(8,128)(2,1)}) %all-gather.12.cloned.1.call-update) | async-done | bytes 12582928 | tf_op jit(solution)/shard_map/all_gather | solution.py:136
  284.2 8.1 fusion.77
  292.3 63.4 %all-gather.14.cloned.1.call-done = bf16[3072,1024]{1,0:T(8,128)(2,1)} async-done(((bf16[96,1024]{1,0:T(8,128)(2,1)}), bf16[3072,1024]{1,0:T(8,128)(2,1)}) %all-gather.14.cloned.1.call-update) | async-done | bytes 6291472 | tf_op jit(solution)/shard_map/all_gather | solution.py:137
  355.7 7.7 multiply_convert_fusion.1
  363.4 7.2 multiply_reduce_fusion.2
  370.7 1.5 subtract_add_fusion
  372.2 4.6 convolution_convert_fusion
  376.7 2.7 copy.188
  379.4 2.9 fusion.48
  382.4 1.3 fusion.53
  383.7 4.2 fusion.6
  387.9 1.2 copy.186
  389.1 2.0 copy.187
  391.3 1.1 maximum_dynamic-update-slice_fusion
  392.5 1.1 slice.129
  393.7 4.5 fusion.57
  399.2 7.5 fusion.89
  406.8 1.0 copy-done.6
  407.7 11.6 fusion.24
  419.6 1.1 mul.787
  420.7 2.6 copy.151
  423.3 1.3 broadcast_bitcast_fusion
  424.5 1.1 mul.754
  425.6 2.5 copy.153
  428.1 1.4 copy.154
  429.6 1.4 copy.161
  431.0 4.4 fusion.7
  435.3 1.5 bitcast_multiply_fusion.9
  437.7 1.3 copy.152
  439.0 2.8 copy.185
  443.3 3.6 multiply_reduce_fusion
  446.9 1.8 convert_bitcast_fusion
  449.6 1.0 fusion.43
  451.4 1.3 broadcast_multiply_fusion.1
  454.0 2.1 fusion.46
  456.8 8.2 fusion.50
  465.0 1.1 copy-done.22
  466.1 4.6 fusion.9
  470.9 6.5 fusion.37
  477.4 40.1 %all-reduce.1 = (f32[1024]{0:T(1024)S(1)}, f32[1024]{0:T(1024)S(1)}, f32[128]{0:T(128)S(1)}, f32[128]{0:T(128)S(1)}) all-reduce(f32[1024]{0:T(1024)S(1)} %get-tuple-element.36, f32[1024]{0:T(1024)S(1)} %copy-done.58, f32[128]{0:T(128)S(1)} %bitcast_reduce_fusion, ...), channel_id=1, replica_groups=mesh['fsdp'=16,'ctx'=2] {'fsdp','ctx'}, use_global_device_ids=true, to_apply=%region_21.22 | all-reduce | flops 2304 | bytes 18432 | tf_op jit(solution)/shard_map/psum | solution.py:271
  519.9 1.0 fusion.34
  520.9 80.5 %reduce-scatter.10.cloned.1.call-done = f32[64,1024]{1,0:T(8,128)} async-done(((f32[2048,1024]{1,0:T(8,128)}), f32[64,1024]{1,0:T(8,128)}) %reduce-scatter.10.cloned.1.call-update) | async-done | bytes 262160 | tf_op jit(solution)/shard_map/reduce_scatter | solution.py:80
  601.4 2.1 multiply_subtract_fusion.3
  603.5 156.3 %reduce-scatter.14.cloned.1.call-done = f32[96,1024]{1,0:T(8,128)} async-done(((f32[3072,1024]{1,0:T(8,128)}), f32[96,1024]{1,0:T(8,128)}) %reduce-scatter.14.cloned.1.call-update) | async-done | bytes 393232 | tf_op jit(solution)/shard_map/reduce_scatter | solution.py:73
  759.9 2.4 multiply_subtract_fusion.2
  762.3 248.6 %reduce-scatter.12.cloned.1.call-done = f32[32,6144]{1,0:T(8,128)} async-done(((f32[1024,6144]{1,0:T(8,128)}), f32[32,6144]{1,0:T(8,128)}) %reduce-scatter.12.cloned.1.call-update) | async-done | bytes 786448 | tf_op jit(solution)/shard_map/reduce_scatter | solution.py:72
  1010.9 2.9 multiply_subtract_fusion
  1013.8 359.6 %reduce-scatter.8.cloned.1.call-done = f32[32,4096]{1,0:T(8,128)} async-done(((f32[1024,4096]{1,0:T(8,128)}), f32[32,4096]{1,0:T(8,128)}) %reduce-scatter.8.cloned.1.call-update) | async-done | bytes 524304 | tf_op jit(solution)/shard_map/reduce_scatter | solution.py:79
  1373.4 2.6 multiply_subtract_fusion.1
  (244 shorter events, 24.3 us)
Async XLA Ops:
  7.2 83.0 %copy-start.12 = (bf16[128,1024]{1,0:T(8,128)(2,1)S(1)}, bf16[128,1024]{1,0:T(8,128)(2,1)}, u32[]{:S(2)}) copy-start(bf16[128,1024]{1,0:T(8,128)(2,1)} %param.27) | copy-start | bytes 786436
  7.2 83.0 %all-gather.6.cloned.1.call-start = ((), (), s32[]{:S(2)}) async-start(), calls=%async_computation.5 | async-start | bytes 8650752 | tf_op jit(solution)/shard_map/all_gather | solution.py:130
  9.1 111.3 %all-gather.8.cloned.1.call-start = ((), (), s32[]{:S(2)}) async-start(), calls=%async_computation.6 | async-start | bytes 1572864 | tf_op jit(solution)/shard_map/all_gather | solution.py:157
  10.0 80.3 %copy-start.72 = (s32[4,1]{0,1:T(1,128)}, s32[4,1]{0,1:T(1,128)S(1)}, u32[]{:S(2)}) copy-start(s32[4,1]{0,1:T(1,128)S(1)} %reduce-window.8) | copy-start | bytes 52
  14.6 80.3 %copy-start.56 = (f32[128]{0:T(128)}, f32[128]{0:T(128)S(1)}, u32[]{:S(2)}) copy-start(f32[128]{0:T(128)S(1)} %get-tuple-element.98) | copy-start | bytes 1540
  95.0 13.3 copy-start.7
  95.0 2.7 copy-start.62
  96.0 4.0 copy-start.10
  100.3 3.3 copy-start.16
  100.9 5.8 copy-start.73
  101.8 85.1 %all-gather.10.cloned.1.call-start = ((), (), s32[]{:S(2)}) async-start(), calls=%async_computation.7 | async-start | bytes 4325376 | tf_op jit(solution)/shard_map/all_gather | solution.py:133
  101.9 3.8 copy-start.30
  103.6 180.7 %all-gather.12.cloned.1.call-start = ((), (), s32[]{:S(2)}) async-start(), calls=%async_computation.8 | async-start | bytes 12976128 | tf_op jit(solution)/shard_map/all_gather | solution.py:136
  105.6 250.2 %all-gather.14.cloned.1.call-start = ((), (), s32[]{:S(2)}) async-start(), calls=%async_computation.9 | async-start | bytes 6488064 | tf_op jit(solution)/shard_map/all_gather | solution.py:137
  106.4 340.5 %reduce-scatter.6.cloned.1.call-start = ((), (), s32[]{:S(2)}) async-start(), calls=%async_computation.10 | async-start | bytes 1572864 | tf_op jit(solution)/shard_map/reduce_scatter | solution.py:247
  110.2 12.2 copy-start.26
  123.4 66.5 %copy-start.51 = (f32[2,8,128]{2,1,0:T(8,128)}, f32[2,8,128]{2,1,0:T(8,128)S(1)}, u32[]{:S(2)}) copy-start(f32[2,8,128]{2,1,0:T(8,128)S(1)} %log_add_fusion) | copy-start | bytes 24580
  124.9 65.1 %copy-start.13 = (bf16[8,128,2,128]{3,1,2,0:T(8,128)(2,1)}, bf16[8,128,2,128]{3,1,2,0:T(8,128)(2,1)S(1)}, u32[]{:S(2)}) copy-start(bf16[8,128,2,128]{3,1,2,0:T(8,128)(2,1)S(1)} %convolution_convert_fusion.1) | copy-start | bytes 1572868
  186.9 97.3 %copy-start.41 = (f32[1024]{0:T(1024)S(1)}, f32[1024]{0:T(1024)}, u32[]{:S(2)}) copy-start(f32[1024]{0:T(1024)} %param.45) | copy-start | bytes 12292
  190.0 102.3 %copy-start.5 = (f32[128,1024]{1,0:T(8,128)}, f32[128,1024]{1,0:T(8,128)S(1)}, u32[]{:S(2)}) copy-start(f32[128,1024]{1,0:T(8,128)S(1)} %get-tuple-element.104) | copy-start | bytes 1572868
  190.6 172.9 %copy-start.55 = (f32[128]{0:T(128)}, f32[128]{0:T(128)S(1)}, u32[]{:S(2)}) copy-start(f32[128]{0:T(128)S(1)} %get-tuple-element.100) | copy-start | bytes 1540
  355.7 7.7 copy-start
  372.2 7.3 copy-start.18
  376.7 5.7 copy-start.2
  379.4 3.0 copy-start.19
  379.4 3.0 copy-start.52
  393.6 207.8 %reduce-scatter.10.cloned.1.call-start = ((), (), s32[]{:S(2)}) async-start(), calls=%async_computation.12 | async-start | bytes 8650752 | tf_op jit(solution)/shard_map/reduce_scatter | solution.py:80
  398.2 361.7 %reduce-scatter.14.cloned.1.call-start = ((), (), s32[]{:S(2)}) async-start(), calls=%async_computation.14 | async-start | bytes 12976128 | tf_op jit(solution)/shard_map/reduce_scatter | solution.py:73
  406.7 604.2 %reduce-scatter.12.cloned.1.call-start = ((), (), s32[]{:S(2)}) async-start(), calls=%async_computation.13 | async-start | bytes 25952256 | tf_op jit(solution)/shard_map/reduce_scatter | solution.py:72
  419.4 954.0 %reduce-scatter.8.cloned.1.call-start = ((), (), s32[]{:S(2)}) async-start(), calls=%async_computation.11 | async-start | bytes 17301504 | tf_op jit(solution)/shard_map/reduce_scatter | solution.py:79
  425.6 5.4 copy-start.53
  439.0 3.1 copy-start.49
  439.0 3.4 copy-start.8
  449.6 4.1 copy-start.48
  453.7 3.1 copy-start.28
  453.7 3.1 copy-start.34
  453.7 3.0 copy-start.42
  453.8 3.0 copy-start.57
  466.1 4.6 copy-start.29
  466.1 4.6 copy-start.33
  466.1 4.6 copy-start.35
  470.8 6.6 copy-start.58
  470.8 46.7 %copy-start.64 = (f32[128]{0:T(128)S(1)}, f32[128]{0:T(128)}, u32[]{:S(2)}) copy-start(f32[128]{0:T(128)} %param.51) | copy-start | bytes 1540
  470.8 46.7 %copy-start.74 = (f32[128]{0:T(128)S(1)}, f32[128]{0:T(128)}, u32[]{:S(2)}) copy-start(f32[128]{0:T(128)} %param.52) | copy-start | bytes 1540
  470.8 46.7 %copy-start.75 = (f32[128]{0:T(128)S(1)}, f32[128]{0:T(128)}, u32[]{:S(2)}) copy-start(f32[128]{0:T(128)} %param.53) | copy-start | bytes 1540
  470.8 47.3 %copy-start.61 = (f32[128]{0:T(128)S(1)}, f32[128]{0:T(128)}, u32[]{:S(2)}) copy-start(f32[128]{0:T(128)} %param.48) | copy-start | bytes 1540
  470.8 47.3 %copy-start.76 = (f32[128]{0:T(128)S(1)}, f32[128]{0:T(128)}, u32[]{:S(2)}) copy-start(f32[128]{0:T(128)} %param.49) | copy-start | bytes 1540
  470.8 47.3 %copy-start.77 = (f32[128]{0:T(128)S(1)}, f32[128]{0:T(128)}, u32[]{:S(2)}) copy-start(f32[128]{0:T(128)} %param.50) | copy-start | bytes 1540
  470.9 47.8 %copy-start.65 = (f32[1024]{0:T(1024)S(1)}, f32[1024]{0:T(1024)}, u32[]{:S(2)}) copy-start(f32[1024]{0:T(1024)} %param.46) | copy-start | bytes 12292
  470.9 47.8 %copy-start.66 = (f32[1024]{0:T(1024)S(1)}, f32[1024]{0:T(1024)}, u32[]{:S(2)}) copy-start(f32[1024]{0:T(1024)} %param.47) | copy-start | bytes 12292
  470.9 48.4 %copy-start.67 = (f32[1024]{0:T(1024)S(1)}, f32[1024]{0:T(1024)}, u32[]{:S(2)}) copy-start(f32[1024]{0:T(1024)} %param.43) | copy-start | bytes 12292
  470.9 48.4 %copy-start.68 = (f32[1024]{0:T(1024)S(1)}, f32[1024]{0:T(1024)}, u32[]{:S(2)}) copy-start(f32[1024]{0:T(1024)} %param.44) | copy-start | bytes 12292
  470.9 49.0 %copy-start.80 = (f32[128]{0:T(128)S(1)}, f32[128]{0:T(128)}, u32[]{:S(2)}) copy-start(f32[128]{0:T(128)} %get-tuple-element.97) | copy-start | bytes 1540
  477.4 124.1 %copy-start.37 = (f32[64,1024]{1,0:T(8,128)S(1)}, f32[64,1024]{1,0:T(8,128)}, u32[]{:S(2)}) copy-start(f32[64,1024]{1,0:T(8,128)} %param.33) | copy-start | bytes 786436
  477.4 282.5 %copy-start.31 = (f32[96,1024]{1,0:T(8,128)S(1)}, f32[96,1024]{1,0:T(8,128)}, u32[]{:S(2)}) copy-start(f32[96,1024]{1,0:T(8,128)} %param.39) | copy-start | bytes 1179652
  517.5 242.3 %copy-start.79 = (f32[128]{0:T(128)}, f32[128]{0:T(128)S(1)}, u32[]{:S(2)}) copy-start(f32[128]{0:T(128)S(1)} %get-tuple-element.43) | copy-start | bytes 1540
  517.5 244.8 %copy-start.69 = (f32[1024]{0:T(1024)}, f32[1024]{0:T(1024)S(1)}, u32[]{:S(2)}) copy-start(f32[1024]{0:T(1024)S(1)} %get-tuple-element.40) | copy-start | bytes 12292
  517.5 244.8 %copy-start.70 = (f32[1024]{0:T(1024)}, f32[1024]{0:T(1024)S(1)}, u32[]{:S(2)}) copy-start(f32[1024]{0:T(1024)S(1)} %get-tuple-element.41) | copy-start | bytes 12292
  517.5 244.8 %copy-start.78 = (f32[128]{0:T(128)}, f32[128]{0:T(128)S(1)}, u32[]{:S(2)}) copy-start(f32[128]{0:T(128)S(1)} %get-tuple-element.42) | copy-start | bytes 1540
  520.9 490.0 %copy-start.23 = (f32[32,6144]{1,0:T(8,128)S(1)}, f32[32,6144]{1,0:T(8,128)}, u32[]{:S(2)}) copy-start(f32[32,6144]{1,0:T(8,128)} %param.36) | copy-start | bytes 2359300
  520.9 490.0 %copy-start.39 = (f32[32,6144]{1,0:T(8,128)S(1)}, f32[32,6144]{1,0:T(8,128)}, u32[]{:S(2)}) copy-start(f32[32,6144]{1,0:T(8,128)} %param.37) | copy-start | bytes 2359300
  520.9 490.0 %copy-start.40 = (f32[32,6144]{1,0:T(8,128)S(1)}, f32[32,6144]{1,0:T(8,128)}, u32[]{:S(2)}) copy-start(f32[32,6144]{1,0:T(8,128)} %param.38) | copy-start | bytes 2359300
  762.3 611.1 %copy-start.24 = (f32[32,4096]{1,0:T(8,128)S(1)}, f32[32,4096]{1,0:T(8,128)}, u32[]{:S(2)}) copy-start(f32[32,4096]{1,0:T(8,128)} %param.30) | copy-start | bytes 1572868
  762.3 611.1 %copy-start.47 = (f32[32,4096]{1,0:T(8,128)S(1)}, f32[32,4096]{1,0:T(8,128)}, u32[]{:S(2)}) copy-start(f32[32,4096]{1,0:T(8,128)} %param.31) | copy-start | bytes 1572868
  (27 other events, 34.1 us)
Sparse Core Ops, SparseCore 0:
  11.6 78.6 all-gather.5
  101.9 18.4 all-gather.7
  124.0 62.9 all-gather.9
  190.3 93.9 all-gather.11
  287.6 68.1 all-gather.13
  393.7 17.4 reduce-scatter.5
  414.1 187.3 reduce-scatter.9
  608.0 151.7 reduce-scatter.13
  766.9 244.0 reduce-scatter.11
  1013.6 359.7 reduce-scatter.7
where the time goes:
time: 1390 us; the launch traced here: 1380 us
  waiting for transfers between devices  1150 us (83%)
  matrix products  92 us (7%)
  other arithmetic  46.4 us (3%)
  blocking collectives  40.1 us (3%)
  local copies, waits for them, and re-layouts  38.9 us (3%)
  between operations  15.4 us (1%)
    reduce_scatter x1, waiting for transfers between devices, reduce_attn(): lax.psum_scatter(grad_qkv, ('fsdp', 'ctx'), scatter_dimension=0, tiled=True)  360 us
    reduce_scatter x1, waiting for transfers between devices, reduce_mlp(): lax.psum_scatter(grad_gateup, ('fsdp', 'ctx'), scatter_dimension=0, tiled...  249 us
    reduce_scatter x1, waiting for transfers between devices, reduce_mlp(): lax.psum_scatter(grad_down, ('fsdp', 'ctx'), scatter_dimension=0, tiled=T...  156 us
    all_gather x1, waiting for transfers between devices, local(): lax.all_gather(w_gateup.astype(jnp.bfloat16), ('fsdp', 'ctx'), axis=0, ti...  93.7 us
    reduce_scatter x1, waiting for transfers between devices, reduce_attn(): lax.psum_scatter(grad_out, ('fsdp', 'ctx'), scatter_dimension=0, tiled=True)  80.5 us
    all_gather x1, waiting for transfers between devices, local(): lax.all_gather(query_key_value_weight.astype(jnp.bfloat16), ('fsdp', 'ctx...  74.9 us
    all_gather x1, waiting for transfers between devices, local(): lax.all_gather(w_down.astype(jnp.bfloat16), ('fsdp', 'ctx'), axis=0, tile...  63.4 us
    all_gather x1, waiting for transfers between devices, local(): lax.all_gather(w_out.astype(jnp.bfloat16), ('fsdp', 'ctx'), axis=0, tiled...  62 us
  transfers between devices with their start and end apart: 10, of which 9 were waited for; matrix products, arithmetic and copies ran while one was open for 8% of the time, Pallas kernels for 0%

commit v1 on v0

--- a/solution.py
+++ b/solution.py
@@ -18,6 +18,27 @@
 MATRIX_RATE = 0.04
 GAIN_RATE = 0.2
 MATRIX_DECAY = 0.1
+
+
+def in_order(blocks, dim):
+    lengths = list(blocks.shape[1:])
+    lengths[dim] *= blocks.shape[0]
+    return jnp.moveaxis(blocks, 0, dim).reshape(lengths)
+
+
+def grow_blocks(x, axis):
+    count, mine = (lax.axis_size(axis), lax.axis_index(axis))
+    blocks, stride = (x[None], 1)
+    while stride < count:
+        other = lax.ppermute(blocks, axis, [(i, i ^ stride) for i in range(count)])
+        low = mine & stride == 0
+        blocks = jnp.concatenate([jnp.where(low, blocks, other), jnp.where(low, other, blocks)])
+        stride *= 2
+    return blocks
+
+
+def gather_by_bits(x, axis, dim):
+    return in_order(grow_blocks(x, axis), dim)
 
 
 def seq_place(lengths, positions):
@@ -133,7 +154,7 @@
         lax.all_gather(w_out.astype(jnp.bfloat16), ("fsdp", "ctx"), axis=0, tiled=True),
     )
     gateup_w, down_w = (
-        lax.all_gather(w_gateup.astype(jnp.bfloat16), ("fsdp", "ctx"), axis=0, tiled=True),
+        gather_by_bits(w_gateup.astype(jnp.bfloat16), ("fsdp", "ctx"), 0),
         lax.all_gather(w_down.astype(jnp.bfloat16), ("fsdp", "ctx"), axis=0, tiled=True),
     )
     tok_float = tokens.astype(jnp.float32)

time: 1390 us -> 1660 us (1.19)
  waiting for transfers between devices: 1150 us -> 1380 us
  other arithmetic: 46.4 us -> 63.9 us
    ppermute x0 -> x5, waiting for transfers between devices: none -> 430 us  [grow_blocks(): other = lax.ppermute(blocks, axis, [(i, i ^ stride) for i in range(count)])]
    reduce_scatter x1, waiting for transfers between devices: 156 us -> 49.3 us  [reduce_mlp(): lax.psum_scatter(grad_down, ('fsdp', 'ctx'), scatter_dimension=0, tiled=T...]
    reduce_scatter x1, waiting for transfers between devices: 80.5 us -> 187 us  [reduce_attn(): lax.psum_scatter(grad_out, ('fsdp', 'ctx'), scatter_dimension=0, tiled=True)]
    all_gather x1, waiting for transfers between devices: 63.4 us -> 0.01 us  [local(): lax.all_gather(w_down.astype(jnp.bfloat16), ('fsdp', 'ctx'), axis=0, tile...]
    all_gather x1, waiting for transfers between devices: 62 us -> 0.01 us  [local(): lax.all_gather(w_out.astype(jnp.bfloat16), ('fsdp', 'ctx'), axis=0, tiled...]
    all_gather x1, waiting for transfers between devices: 93.7 us -> 33 us  [local(): lax.all_gather(w_gateup.astype(jnp.bfloat16), ('fsdp', 'ctx'), axis=0, ti...]
  transfers between devices with their start and end apart: 10 -> 15, of which waited for: 9 -> 11; matrix products, arithmetic and copies ran while one was open for 8% -> 9% of each run, Pallas kernels for 0% -> 0%
where the time goes in v1:
time: 1660 us; the launch traced here: 1650 us
  waiting for transfers between devices  1380 us (83%)
  matrix products  101 us (6%)
  other arithmetic  63.9 us (4%)
  blocking collectives  41.8 us (3%)
  local copies, waits for them, and re-layouts  41.2 us (2%)
    ppermute x5, waiting for transfers between devices, grow_blocks(): other = lax.ppermute(blocks, axis, [(i, i ^ stride) for i in range(count)])  430 us
    reduce_scatter x1, waiting for transfers between devices, reduce_attn(): lax.psum_scatter(grad_qkv, ('fsdp', 'ctx'), scatter_dimension=0, tiled=True)  360 us
    reduce_scatter x1, waiting for transfers between devices, reduce_mlp(): lax.psum_scatter(grad_gateup, ('fsdp', 'ctx'), scatter_dimension=0, tiled...  247 us
    reduce_scatter x1, waiting for transfers between devices, reduce_attn(): lax.psum_scatter(grad_out, ('fsdp', 'ctx'), scatter_dimension=0, tiled=True)  187 us
    all_gather x1, waiting for transfers between devices, local(): lax.all_gather(query_key_value_weight.astype(jnp.bfloat16), ('fsdp', 'ctx...  74.9 us
    reduce_scatter x1, waiting for transfers between devices, reduce_mlp(): lax.psum_scatter(grad_down, ('fsdp', 'ctx'), scatter_dimension=0, tiled=T...  49.3 us
    psum x1, blocking collectives, local(): lax.psum((gain_one, gain_two, gain_q, gain_k), ('fsdp', 'ctx'))  41.8 us
  transfers between devices with their start and end apart: 15, of which 11 were waited for; matrix products, arithmetic and copies ran while one was open for 9% of the time, Pallas kernels for 0%

profile of v1, /device:TPU:11, one launch (start us, length us, event | category | flops | bytes accessed | tf_op | source)
XLA Modules:
  0.0 1648.8 jit_solution(7627294572984580907)
XLA Ops:
  7.3 1.8 convert_element_type.83
  10.0 1.2 fusion.66
  15.3 74.9 %all-gather.6.cloned.1.call-done = bf16[1024,4096]{1,0:T(8,128)(2,1)} async-done(((bf16[32,4096]{1,0:T(8,128)(2,1)}), bf16[1024,4096]{1,0:T(8,128)(2,1)}) %all-gather.6.cloned.1.call-update) | async-done | bytes 8388624 | tf_op jit(solution)/shard_map/all_gather | solution.py:151
  90.3 4.7 fusion.61
  104.0 14.7 collective-permute-done
  119.6 2.5 collective-permute-start.1
  123.0 1.2 collective-permute-done.1
  124.2 1.3 broadcast_select_fusion.7
  125.8 38.5 %collective-permute-done.2 = bf16[4,32,6144]{2,1,0:T(8,128)(2,1)} collective-permute-done((bf16[4,32,6144]{2,1,0:T(8,128)(2,1)S(1)}, bf16[4,32,6144]{2,1,0:T(8,128)(2,1)}, u32[]{:S(2)}, u32[]{:S(2)}) %collective-permute-start.2) | collective-permute-done | bytes 1572896 | tf_op jit(solution)/shard_map/ppermute | solution.py:33
  164.3 1.6 broadcast_select_fusion.5
  168.0 96.6 %collective-permute-done.3 = bf16[8,32,6144]{2,1,0:T(8,128)(2,1)} collective-permute-done((bf16[8,32,6144]{2,1,0:T(8,128)(2,1)S(1)}, bf16[8,32,6144]{2,1,0:T(8,128)(2,1)}, u32[]{:S(2)}, u32[]{:S(2)}) %collective-permute-start.3) | collective-permute-done | bytes 3145760 | tf_op jit(solution)/shard_map/ppermute | solution.py:33
  264.6 3.0 broadcast_select_fusion.3
  267.7 3.4 pad_maximum_fusion.1
  272.4 1.4 compare_and_fusion
  273.8 279.0 %collective-permute-done.4 = bf16[16,32,6144]{2,1,0:T(8,128)(2,1)} collective-permute-done((bf16[16,32,6144]{2,1,0:T(8,128)(2,1)}, bf16[16,32,6144]{2,1,0:T(8,128)(2,1)}, u32[]{:S(2)}, u32[]{:S(2)}) %collective-permute-start.4) | collective-permute-done | bytes 6291488 | tf_op jit(solution)/shard_map/ppermute | solution.py:33
  552.9 4.5 broadcast_select_fusion.1
  557.3 5.8 pad_maximum_fusion
  563.1 1.2 slice-done
  566.8 1.4 fusion.38
  568.3 1.1 copy.170
  569.5 1.9 fusion.88
  572.4 1.3 convolution_convert_fusion.1
  573.7 3.2 multiply_reduce_fusion.5
  578.0 8.1 fusion.77
  586.1 9.3 multiply_convert_fusion.1
  595.4 33.0 %all-gather.14.cloned.1.call-done = bf16[1024,6144]{1,0:T(8,128)(2,1)} async-done(((bf16[32,6144]{1,0:T(8,128)(2,1)}), bf16[1024,6144]{1,0:T(8,128)(2,1)}) %all-gather.14.cloned.1.call-update) | async-done | bytes 12582928 | tf_op jit(solution)/shard_map/all_gather | solution.py:221
  628.4 10.4 multiply_reduce_fusion.2
  639.7 2.3 convolution_convert_fusion
  642.0 2.1 copy.188
  644.1 3.2 fusion.48
  647.3 1.3 fusion.53
  648.6 4.1 fusion.6
  652.7 2.0 copy.186
  654.7 2.0 copy.187
  656.9 1.3 maximum_dynamic-update-slice_fusion
  658.3 1.1 slice.129
  659.5 7.6 fusion.89
  667.1 5.7 fusion.57
  672.9 13.4 fusion.24
  687.6 2.6 copy.151
  690.2 1.3 broadcast_bitcast_fusion
  692.6 2.6 copy.153
  695.2 1.4 copy.154
  696.6 1.4 copy.161
  698.0 4.6 fusion.7
  702.7 1.4 bitcast_multiply_fusion.9
  704.8 1.3 copy.152
  706.1 1.3 copy.185
  709.2 3.7 multiply_reduce_fusion
  712.9 1.9 convert_bitcast_fusion
  717.5 1.3 broadcast_multiply_fusion.1
  720.1 1.9 fusion.46
  722.7 8.9 fusion.50
  732.9 4.6 fusion.9
  737.7 6.5 fusion.37
  744.1 41.8 %all-reduce.1 = (f32[1024]{0:T(1024)S(1)}, f32[1024]{0:T(1024)S(1)}, f32[128]{0:T(128)S(1)}, f32[128]{0:T(128)S(1)}) all-reduce(f32[1024]{0:T(1024)S(1)} %get-tuple-element.36, f32[1024]{0:T(1024)S(1)} %copy-done.60, f32[128]{0:T(128)S(1)} %bitcast_reduce_fusion, ...), channel_id=1, replica_groups=mesh['fsdp'=16,'ctx'=2] {'fsdp','ctx'}, use_global_device_ids=true, to_apply=%region_21.22 | all-reduce | flops 2304 | bytes 18432 | tf_op jit(solution)/shard_map/psum | solution.py:292
  789.4 49.3 %reduce-scatter.14.cloned.1.call-done = f32[96,1024]{1,0:T(8,128)} async-done(((f32[3072,1024]{1,0:T(8,128)}), f32[96,1024]{1,0:T(8,128)}) %reduce-scatter.14.cloned.1.call-update) | async-done | bytes 393232 | tf_op jit(solution)/shard_map/reduce_scatter | solution.py:94
  838.7 2.4 multiply_subtract_fusion.2
  841.1 186.6 %reduce-scatter.10.cloned.1.call-done = f32[64,1024]{1,0:T(8,128)} async-done(((f32[2048,1024]{1,0:T(8,128)}), f32[64,1024]{1,0:T(8,128)}) %reduce-scatter.10.cloned.1.call-update) | async-done | bytes 262160 | tf_op jit(solution)/shard_map/reduce_scatter | solution.py:101
  1027.8 2.0 multiply_subtract_fusion.3
  1029.8 246.9 %reduce-scatter.12.cloned.1.call-done = f32[32,6144]{1,0:T(8,128)} async-done(((f32[1024,6144]{1,0:T(8,128)}), f32[32,6144]{1,0:T(8,128)}) %reduce-scatter.12.cloned.1.call-update) | async-done | bytes 786448 | tf_op jit(solution)/shard_map/reduce_scatter | solution.py:93
  1276.7 2.9 multiply_subtract_fusion
  1279.6 359.6 %reduce-scatter.8.cloned.1.call-done = f32[32,4096]{1,0:T(8,128)} async-done(((f32[1024,4096]{1,0:T(8,128)}), f32[32,4096]{1,0:T(8,128)}) %reduce-scatter.8.cloned.1.call-update) | async-done | bytes 524304 | tf_op jit(solution)/shard_map/reduce_scatter | solution.py:100
  1639.2 2.6 multiply_subtract_fusion.1
  (272 shorter events, 39.4 us)
Async XLA Ops:
  7.2 83.0 %copy-start.16 = (bf16[128,1024]{1,0:T(8,128)(2,1)S(1)}, bf16[128,1024]{1,0:T(8,128)(2,1)}, u32[]{:S(2)}) copy-start(bf16[128,1024]{1,0:T(8,128)(2,1)} %param.27) | copy-start | bytes 786436
  7.2 83.0 %all-gather.6.cloned.1.call-start = ((), (), s32[]{:S(2)}) async-start(), calls=%async_computation.5 | async-start | bytes 8650752 | tf_op jit(solution)/shard_map/all_gather | solution.py:151
  9.1 557.7 %all-gather.8.cloned.1.call-start = ((), (), s32[]{:S(2)}) async-start(), calls=%async_computation.6 | async-start | bytes 1572864 | tf_op jit(solution)/shard_map/all_gather | solution.py:178
  10.0 80.3 %copy-start.74 = (s32[4,1]{0,1:T(1,128)}, s32[4,1]{0,1:T(1,128)S(1)}, u32[]{:S(2)}) copy-start(s32[4,1]{0,1:T(1,128)S(1)} %reduce-window.8) | copy-start | bytes 52
  14.6 80.3 %copy-start.58 = (f32[128]{0:T(128)}, f32[128]{0:T(128)S(1)}, u32[]{:S(2)}) copy-start(f32[128]{0:T(128)S(1)} %get-tuple-element.108) | copy-start | bytes 1540
  95.0 5.3 copy-start.4
  96.0 4.0 copy-start.12
  100.3 3.3 copy-start.9
  102.0 471.7 %all-gather.10.cloned.1.call-start = ((), (), s32[]{:S(2)}) async-start(), calls=%async_computation.7 | async-start | bytes 4325376 | tf_op jit(solution)/shard_map/all_gather | solution.py:154
  102.7 483.4 %all-gather.12.cloned.1.call-start = ((), (), s32[]{:S(2)}) async-start(), calls=%async_computation.8 | async-start | bytes 6488064 | tf_op jit(solution)/shard_map/all_gather | solution.py:158
  103.5 524.8 %all-gather.14.cloned.1.call-start = ((), (), s32[]{:S(2)}) async-start(), calls=%async_computation.9 | async-start | bytes 12976128 | tf_op jit(solution)/shard_map/all_gather | solution.py:221
  103.6 15.1 collective-permute-start
  119.6 4.6 collective-permute-start.1
  123.0 589.9 %reduce-scatter.6.cloned.1.call-start = ((), (), s32[]{:S(2)}) async-start(), calls=%async_computation.10 | async-start | bytes 1572864 | tf_op jit(solution)/shard_map/reduce_scatter | solution.py:268
  125.7 38.6 %collective-permute-start.2 = (bf16[4,32,6144]{2,1,0:T(8,128)(2,1)S(1)}, bf16[4,32,6144]{2,1,0:T(8,128)(2,1)}, u32[]{:S(2)}, u32[]{:S(2)}) collective-permute-start(bf16[4,32,6144]{2,1,0:T(8,128)(2,1)S(1)} %pad_maximum_fusion.3), channel_id=1, source_target_pairs={{0,4},{1,5},{2,6},{3,7},{4,0},{5,1},{6,2},{7,3},{8,12},{9,13},{10,... | collective-permute-start | bytes 4718600 | tf_op jit(solution)/shard_map/ppermute | solution.py:33
  167.6 97.1 %collective-permute-start.3 = (bf16[8,32,6144]{2,1,0:T(8,128)(2,1)S(1)}, bf16[8,32,6144]{2,1,0:T(8,128)(2,1)}, u32[]{:S(2)}, u32[]{:S(2)}) collective-permute-start(bf16[8,32,6144]{2,1,0:T(8,128)(2,1)S(1)} %pad_maximum_fusion.2), channel_id=1, source_target_pairs={{0,8},{1,9},{2,10},{3,11},{4,12},{5,13},{6,14},{7,15},{8,0},{9,1},... | collective-permute-start | bytes 9437192 | tf_op jit(solution)/shard_map/ppermute | solution.py:33
  267.7 3.6 copy-start
  267.7 4.6 copy-start.75
  271.3 281.6 %collective-permute-start.4 = (bf16[16,32,6144]{2,1,0:T(8,128)(2,1)}, bf16[16,32,6144]{2,1,0:T(8,128)(2,1)}, u32[]{:S(2)}, u32[]{:S(2)}) collective-permute-start(bf16[16,32,6144]{2,1,0:T(8,128)(2,1)} %pad_maximum_fusion.1), channel_id=1, source_target_pairs={{0,16},{1,17},{2,18},{3,19},{4,20},{5,21},{6,22},{7,23},{8,24},{9,... | collective-permute-start | bytes 18874376 | tf_op jit(solution)/shard_map/ppermute | solution.py:33
  573.7 4.3 copy-start.42
  628.4 10.4 copy-start.2
  628.4 10.4 copy-start.36
  628.4 10.4 copy-start.57
  628.4 10.4 copy-start.83
  628.4 11.4 copy-start.6
  644.1 3.2 copy-start.22
  644.1 3.2 copy-start.53
  659.4 179.3 %reduce-scatter.14.cloned.1.call-start = ((), (), s32[]{:S(2)}) async-start(), calls=%async_computation.14 | async-start | bytes 12976128 | tf_op jit(solution)/shard_map/reduce_scatter | solution.py:94
  667.0 360.7 %reduce-scatter.10.cloned.1.call-start = ((), (), s32[]{:S(2)}) async-start(), calls=%async_computation.12 | async-start | bytes 8650752 | tf_op jit(solution)/shard_map/reduce_scatter | solution.py:101
  672.8 603.8 %reduce-scatter.12.cloned.1.call-start = ((), (), s32[]{:S(2)}) async-start(), calls=%async_computation.13 | async-start | bytes 25952256 | tf_op jit(solution)/shard_map/reduce_scatter | solution.py:93
  686.3 952.8 %reduce-scatter.8.cloned.1.call-start = ((), (), s32[]{:S(2)}) async-start(), calls=%async_computation.11 | async-start | bytes 17301504 | tf_op jit(solution)/shard_map/reduce_scatter | solution.py:100
  692.6 5.5 copy-start.54
  715.7 4.2 copy-start.50
  715.7 4.4 copy-start.18
  715.7 4.4 copy-start.20
  719.8 2.8 copy-start.28
  732.9 4.6 copy-start.29
  732.9 4.6 copy-start.33
  732.9 4.6 copy-start.35
  737.5 6.6 copy-start.60
  737.5 48.5 %copy-start.66 = (f32[128]{0:T(128)S(1)}, f32[128]{0:T(128)}, u32[]{:S(2)}) copy-start(f32[128]{0:T(128)} %param.51) | copy-start | bytes 1540
  737.5 48.5 %copy-start.76 = (f32[128]{0:T(128)S(1)}, f32[128]{0:T(128)}, u32[]{:S(2)}) copy-start(f32[128]{0:T(128)} %param.52) | copy-start | bytes 1540
  737.5 48.5 %copy-start.77 = (f32[128]{0:T(128)S(1)}, f32[128]{0:T(128)}, u32[]{:S(2)}) copy-start(f32[128]{0:T(128)} %param.53) | copy-start | bytes 1540
  737.6 49.0 %copy-start.63 = (f32[128]{0:T(128)S(1)}, f32[128]{0:T(128)}, u32[]{:S(2)}) copy-start(f32[128]{0:T(128)} %param.48) | copy-start | bytes 1540
  737.6 49.0 %copy-start.78 = (f32[128]{0:T(128)S(1)}, f32[128]{0:T(128)}, u32[]{:S(2)}) copy-start(f32[128]{0:T(128)} %param.49) | copy-start | bytes 1540
  737.6 49.0 %copy-start.79 = (f32[128]{0:T(128)S(1)}, f32[128]{0:T(128)}, u32[]{:S(2)}) copy-start(f32[128]{0:T(128)} %param.50) | copy-start | bytes 1540
  737.6 49.5 %copy-start.67 = (f32[1024]{0:T(1024)S(1)}, f32[1024]{0:T(1024)}, u32[]{:S(2)}) copy-start(f32[1024]{0:T(1024)} %param.46) | copy-start | bytes 12292
  737.6 49.5 %copy-start.68 = (f32[1024]{0:T(1024)S(1)}, f32[1024]{0:T(1024)}, u32[]{:S(2)}) copy-start(f32[1024]{0:T(1024)} %param.47) | copy-start | bytes 12292
  737.6 50.1 %copy-start.69 = (f32[1024]{0:T(1024)S(1)}, f32[1024]{0:T(1024)}, u32[]{:S(2)}) copy-start(f32[1024]{0:T(1024)} %param.43) | copy-start | bytes 12292
  737.6 50.1 %copy-start.70 = (f32[1024]{0:T(1024)S(1)}, f32[1024]{0:T(1024)}, u32[]{:S(2)}) copy-start(f32[1024]{0:T(1024)} %param.44) | copy-start | bytes 12292
  737.6 50.7 %copy-start.15 = (f32[128,1024]{1,0:T(8,128)S(1)}, f32[128,1024]{1,0:T(8,128)}, u32[]{:S(2)}) copy-start(f32[128,1024]{1,0:T(8,128)} %copy-done.14) | copy-start | bytes 1572868
  737.7 50.7 %copy-start.82 = (f32[128]{0:T(128)S(1)}, f32[128]{0:T(128)}, u32[]{:S(2)}) copy-start(f32[128]{0:T(128)} %get-tuple-element.107) | copy-start | bytes 1540
  744.1 94.6 %copy-start.31 = (f32[96,1024]{1,0:T(8,128)S(1)}, f32[96,1024]{1,0:T(8,128)}, u32[]{:S(2)}) copy-start(f32[96,1024]{1,0:T(8,128)} %param.39) | copy-start | bytes 1179652
  786.0 55.1 %copy-start.71 = (f32[1024]{0:T(1024)}, f32[1024]{0:T(1024)S(1)}, u32[]{:S(2)}) copy-start(f32[1024]{0:T(1024)S(1)} %get-tuple-element.40) | copy-start | bytes 12292
  786.0 55.1 %copy-start.72 = (f32[1024]{0:T(1024)}, f32[1024]{0:T(1024)S(1)}, u32[]{:S(2)}) copy-start(f32[1024]{0:T(1024)S(1)} %get-tuple-element.41) | copy-start | bytes 12292
  786.0 55.1 %copy-start.80 = (f32[128]{0:T(128)}, f32[128]{0:T(128)S(1)}, u32[]{:S(2)}) copy-start(f32[128]{0:T(128)S(1)} %get-tuple-element.42) | copy-start | bytes 1540
  786.0 55.1 %copy-start.81 = (f32[128]{0:T(128)}, f32[128]{0:T(128)S(1)}, u32[]{:S(2)}) copy-start(f32[128]{0:T(128)S(1)} %get-tuple-element.43) | copy-start | bytes 1540
  788.4 239.4 %copy-start.38 = (f32[64,1024]{1,0:T(8,128)S(1)}, f32[64,1024]{1,0:T(8,128)}, u32[]{:S(2)}) copy-start(f32[64,1024]{1,0:T(8,128)} %param.33) | copy-start | bytes 786436
  789.4 238.4 %copy-start.49 = (f32[64,1024]{1,0:T(8,128)S(1)}, f32[64,1024]{1,0:T(8,128)}, u32[]{:S(2)}) copy-start(f32[64,1024]{1,0:T(8,128)} %param.34) | copy-start | bytes 786436
  789.4 487.3 %copy-start.10 = (f32[32,6144]{1,0:T(8,128)S(1)}, f32[32,6144]{1,0:T(8,128)}, u32[]{:S(2)}) copy-start(f32[32,6144]{1,0:T(8,128)} %param.36) | copy-start | bytes 2359300
  789.4 487.3 %copy-start.40 = (f32[32,6144]{1,0:T(8,128)S(1)}, f32[32,6144]{1,0:T(8,128)}, u32[]{:S(2)}) copy-start(f32[32,6144]{1,0:T(8,128)} %param.37) | copy-start | bytes 2359300
  789.4 487.3 %copy-start.41 = (f32[32,6144]{1,0:T(8,128)S(1)}, f32[32,6144]{1,0:T(8,128)}, u32[]{:S(2)}) copy-start(f32[32,6144]{1,0:T(8,128)} %param.38) | copy-start | bytes 2359300
  1029.8 609.4 %copy-start.27 = (f32[32,4096]{1,0:T(8,128)S(1)}, f32[32,4096]{1,0:T(8,128)}, u32[]{:S(2)}) copy-start(f32[32,4096]{1,0:T(8,128)} %param.30) | copy-start | bytes 1572868
  1029.8 609.4 %copy-start.48 = (f32[32,4096]{1,0:T(8,128)S(1)}, f32[32,4096]{1,0:T(8,128)}, u32[]{:S(2)}) copy-start(f32[32,4096]{1,0:T(8,128)} %param.31) | copy-start | bytes 1572868
  (36 other events, 52.6 us)
Sparse Core Ops, SparseCore 0:
  11.6 78.6 all-gather.5
  102.1 24.0 all-gather.7
  129.7 70.0 all-gather.9
  203.2 78.5 all-gather.11
  285.1 343.1 all-gather.13
  659.5 17.7 reduce-scatter.5
  683.9 154.7 reduce-scatter.13
  841.5 186.1 reduce-scatter.9
  1034.8 241.8 reduce-scatter.11
  1279.4 359.7 reduce-scatter.7
